TPU v7x, 32 devices: a whole 2x2x4 slice. The times are simulated.
32 devices in a mesh: groups: 1, ex: 16 (over z, y, core), layer: 2 (over x), pb: 1.
Axes of the slice: x: 2, y: 2, z: 4, core: 2. Of those that a mesh axis runs over, the one named last changes fastest.
Arguments:
- train_grads: float32 [2, 1536, 1024], P('layer', ('groups', 'ex')), may hold values from -64 to 64
- query_grads: float32 [2, 1, 512, 1024], P('layer', 'pb', ('groups', 'ex')), may hold values from -64 to 64
- damping: float32 [2], P('layer'), may hold values from 0.05 to 0.5
Outputs:
- influence: float32 [1536, 1, 512], P(('groups', 'ex'), 'pb', 'layer')
All inputs are finite; a program needn't handle non-finite values.
Results may differ from a plain program's by a relative error of at most 0.0003.
Values sent between devices are 32-bit elements; how exact they have to be, the bound alone decides.
A program may use at most 64 MiB of HBM per device.

v0:
```python
import jax
import jax.numpy as jnp
from jax import lax
from jax.sharding import PartitionSpec as P


def solve_rows(factor, rows_in):
    inner = lax.linalg.triangular_solve(
        factor, rows_in, left_side=False, lower=True, transpose_a=True
    )
    return lax.linalg.triangular_solve(
        factor, inner, left_side=False, lower=True, transpose_a=False
    )


def on_device(train_grads, query_grads, damping):
    layers_here, local_rows, coords = train_grads.shape
    total_rows = local_rows * lax.axis_size("ex")
    half_rows = local_rows // lax.axis_size("pb")
    own_rows = lax.dynamic_slice_in_dim(train_grads, lax.axis_index("pb") * half_rows, half_rows, 1)
    partial_gram = jnp.einsum("lnp,lnq->lpq", own_rows, own_rows, precision=lax.Precision.HIGHEST)
    gram_matrix = lax.psum(partial_gram, ("ex", "pb"))
    identity = jnp.eye(coords, dtype=jnp.float32)
    fisher = gram_matrix / total_rows + damping[:, None, None] * identity[None]
    factor = jnp.linalg.cholesky(fisher)
    queries = query_grads[:, 0]
    solved = solve_rows(factor, queries)
    score_tile = jnp.einsum(
        "lnp,lkp->nk",
        train_grads,
        lax.all_gather(solved, "ex", axis=1, tiled=True),
        precision=lax.Precision.HIGHEST,
    )
    shares = lax.psum_scatter(score_tile, "layer", scatter_dimension=1, tiled=True)
    return shares[:, None, :]


def solution(mesh):
    in_specs = (
        P("layer", ("groups", "ex"), None),
        P("layer", "pb", ("groups", "ex"), None),
        P("layer"),
    )
    out_specs = P(("groups", "ex"), "pb", "layer")
    return jax.shard_map(
        on_device, mesh=mesh, in_specs=in_specs, out_specs=out_specs, check_vma=False
    )
```

profile of v0, /device:TPU:0, one launch (start us, length us, event | category | flops | bytes accessed | tf_op | source)
XLA Modules:
  0.0 545.7 jit_solution(9678609055191033883)
XLA Ops:
  7.5 5.0 convolution_bitcast_fusion
  13.3 113.3 %all-reduce.3.cloned.1.call-done = f32[1,1024,1024]{1,2,0:T(8,128)} async-done(((f32[1,1024,1024]{1,2,0:T(8,128)}), f32[1,1024,1024]{1,2,0:T(8,128)}) %all-reduce.3.cloned.1.call-update) | async-done | bytes 4194320 | tf_op jit(solution)/shard_map/psum | solution.py:22
  126.6 5.1 select_add_fusion
  131.7 5.6 %copy.5 = f32[1,1024,1024]{2,1,0:T(8,128)} copy(f32[1,1024,1024]{1,2,0:T(8,128)} %select_add_fusion) | data formatting | bytes 8388608 | tf_op jit(solution)/shard_map/add | solution.py:24
  137.3 4.5 fusion
  141.8 1.9 copy-done.1
  143.7 11.7 %custom-call.72 = f32[1,128,128]{2,1,0:T(8,128)S(1)} custom-call(f32[1,128,128]{2,1,0:T(8,128)S(1)} %cholesky.582), custom_call_target="Cholesky" | custom-call | tf_op jit(solution)/shard_map/jit(cholesky)/cholesky | solution.py:25
  155.6 9.8 %custom-call.73 = f32[1,1,128,128]{2,3,1,0:T(8,128)S(1)} custom-call(f32[1,1,128,128]{3,2,1,0:T(8,128)S(1)} %get-tuple-element.40), custom_call_target="InvertDiagBlocksLowerTriangular" | custom-call | tf_op jit(solution)/shard_map/jit(cholesky)/cholesky | solution.py:25
  165.4 1.5 fusion.34
  167.1 1.5 fusion.3
  168.7 11.7 %custom-call.74 = f32[1,128,128]{2,1,0:T(8,128)S(1)} custom-call(f32[1,128,128]{2,1,0:T(8,128)S(1)} %cholesky.586), custom_call_target="Cholesky" | custom-call | tf_op jit(solution)/shard_map/jit(cholesky)/cholesky | solution.py:25
  181.1 2.5 cholesky.248
  184.4 9.8 %custom-call.75 = f32[1,1,128,128]{2,3,1,0:T(8,128)S(1)} custom-call(f32[1,1,128,128]{3,2,1,0:T(8,128)S(1)} %get-tuple-element.38), custom_call_target="InvertDiagBlocksLowerTriangular" | custom-call | tf_op jit(solution)/shard_map/jit(cholesky)/cholesky | solution.py:25
  196.1 2.7 fusion.6
  198.9 11.7 %custom-call.76 = f32[1,128,128]{2,1,0:T(8,128)S(1)} custom-call(f32[1,128,128]{2,1,0:T(8,128)S(1)} %cholesky.591), custom_call_target="Cholesky" | custom-call | tf_op jit(solution)/shard_map/jit(cholesky)/cholesky | solution.py:25
  211.3 9.8 %custom-call.77 = f32[1,1,128,128]{2,3,1,0:T(8,128)S(1)} custom-call(f32[1,1,128,128]{3,2,1,0:T(8,128)S(1)} %get-tuple-element.36), custom_call_target="InvertDiagBlocksLowerTriangular" | custom-call | tf_op jit(solution)/shard_map/jit(cholesky)/cholesky | solution.py:25
  222.4 3.3 fusion.8
  225.7 11.7 %custom-call.78 = f32[1,128,128]{2,1,0:T(8,128)S(1)} custom-call(f32[1,128,128]{2,1,0:T(8,128)S(1)} %cholesky.596), custom_call_target="Cholesky" | custom-call | tf_op jit(solution)/shard_map/jit(cholesky)/cholesky | solution.py:25
  238.2 9.8 %custom-call.79 = f32[1,1,128,128]{2,3,1,0:T(8,128)S(1)} custom-call(f32[1,1,128,128]{3,2,1,0:T(8,128)S(1)} %get-tuple-element.34), custom_call_target="InvertDiagBlocksLowerTriangular" | custom-call | tf_op jit(solution)/shard_map/jit(cholesky)/cholesky | solution.py:25
  249.2 3.1 fusion.9
  252.3 11.9 %custom-call.80 = f32[1,128,128]{2,1,0:T(8,128)S(1)} custom-call(f32[1,128,128]{2,1,0:T(8,128)S(1)} %cholesky.601), custom_call_target="Cholesky" | custom-call | tf_op jit(solution)/shard_map/jit(cholesky)/cholesky | solution.py:25
  265.0 9.8 %custom-call.81 = f32[1,1,128,128]{2,3,1,0:T(8,128)S(1)} custom-call(f32[1,1,128,128]{3,2,1,0:T(8,128)S(1)} %get-tuple-element.32), custom_call_target="InvertDiagBlocksLowerTriangular" | custom-call | tf_op jit(solution)/shard_map/jit(cholesky)/cholesky | solution.py:25
  275.9 3.1 fusion.14
  279.0 11.7 %custom-call.82 = f32[1,128,128]{2,1,0:T(8,128)S(1)} custom-call(f32[1,128,128]{2,1,0:T(8,128)S(1)} %cholesky.606), custom_call_target="Cholesky" | custom-call | tf_op jit(solution)/shard_map/jit(cholesky)/cholesky | solution.py:25
  291.5 9.8 %custom-call.83 = f32[1,1,128,128]{2,3,1,0:T(8,128)S(1)} custom-call(f32[1,1,128,128]{3,2,1,0:T(8,128)S(1)} %get-tuple-element.30), custom_call_target="InvertDiagBlocksLowerTriangular" | custom-call | tf_op jit(solution)/shard_map/jit(cholesky)/cholesky | solution.py:25
  302.3 3.1 fusion.16
  305.4 11.7 %custom-call.84 = f32[1,128,128]{2,1,0:T(8,128)S(1)} custom-call(f32[1,128,128]{2,1,0:T(8,128)S(1)} %cholesky.611), custom_call_target="Cholesky" | custom-call | tf_op jit(solution)/shard_map/jit(cholesky)/cholesky | solution.py:25
  317.9 9.8 %custom-call.85 = f32[1,1,128,128]{2,3,1,0:T(8,128)S(1)} custom-call(f32[1,1,128,128]{3,2,1,0:T(8,128)S(1)} %get-tuple-element.28), custom_call_target="InvertDiagBlocksLowerTriangular" | custom-call | tf_op jit(solution)/shard_map/jit(cholesky)/cholesky | solution.py:25
  328.6 2.1 fusion.18
  330.7 11.7 %custom-call.86 = f32[1,128,128]{2,1,0:T(8,128)S(1)} custom-call(f32[1,128,128]{2,1,0:T(8,128)S(1)} %fusion.18), custom_call_target="Cholesky" | custom-call | tf_op jit(solution)/shard_map/jit(cholesky)/cholesky | solution.py:25
  352.9 4.9 select_select_fusion
  357.8 23.7 %while.1 = (s32[]{:T(128)}, f32[1,1024,1024]{1,2,0:T(8,128)}, s32[8,2]{0,1:T(2,128)S(1)}, f32[8,1,128,128]{3,2,1,0:T(8,128)S(1)}, s32[]{:T(128)}) while((s32[]{:T(128)}, f32[1,1024,1024]{1,2,0:T(8,128)}, s32[8,2]{0,1:T(2,128)S(1)}, f32[8,1,128,128]{3,2,1,0:T(8,128)S(1)}, s32[]{:T(128)}) %tuple.49), condition=%wide.while_cond, body=%wide.while_body.sunk | while | flops 2 | bytes 393333 | solution.py:8
  358.4 2.2 constant_dynamic-slice_fusion.5
  361.4 2.2 constant_dynamic-slice_fusion.5
  364.4 2.2 constant_dynamic-slice_fusion.5
  367.3 2.2 constant_dynamic-slice_fusion.5
  370.3 2.2 constant_dynamic-slice_fusion.5
  373.3 2.2 constant_dynamic-slice_fusion.5
  376.3 2.2 constant_dynamic-slice_fusion.5
  379.3 2.2 constant_dynamic-slice_fusion.5
  381.5 78.8 %custom-call.87 = f32[1,8,128,128]{2,3,1,0:T(8,128)S(1)} custom-call(f32[1,8,128,128]{3,2,1,0:T(8,128)S(1)} %bitcast.460), custom_call_target="InvertDiagBlocksLowerTriangular" | custom-call | tf_op jit(solution)/shard_map/triangular_solve | solution.py:8
  468.7 1.4 fusion.29
  477.9 1.5 convolution_subtract_fusion.5
  479.7 1.6 convolution_subtract_fusion.4
  482.3 40.7 %all-gather.2.cloned.1.call-done = f32[1,512,1024]{2,1,0:T(8,128)} async-done(((f32[1,32,1024]{2,1,0:T(8,128)}), f32[1,512,1024]{2,1,0:T(8,128)}) %all-gather.2.cloned.1.call-update) | async-done | bytes 2097168 | tf_op jit(solution)/shard_map/all_gather | solution.py:31
  523.0 4.4 fusion.10
  527.5 9.9 %reduce-scatter.2.cloned.1.call-done = f32[96,256]{1,0:T(8,128)} async-done(((f32[96,512]{1,0:T(8,128)}), f32[96,256]{1,0:T(8,128)}) %reduce-scatter.2.cloned.1.call-update) | async-done | bytes 98320 | tf_op jit(solution)/shard_map/reduce_scatter | solution.py:34
  537.4 1.6 copy.22
  (142 shorter events, 42.5 us)
Async XLA Ops:
  6.5 1.0 copy-start
  6.5 120.0 %all-reduce.3.cloned.1.call-start = ((), (), s32[]{:S(2)}) async-start(), calls=%async_computation.1 | async-start | bytes 8388608 | tf_op jit(solution)/shard_map/psum | solution.py:22
  12.6 510.4 %all-gather.2.cloned.1.call-start = ((), (), s32[]{:S(2)}) async-start(), calls=%async_computation.2 | async-start | bytes 2228224 | tf_op jit(solution)/shard_map/all_gather | solution.py:31
  141.8 1.9 copy-start.1
  352.9 107.4 %copy-start.3 = (f32[1,1,32,1024]{3,2,1,0:T(8,128)S(1)}, f32[1,1,32,1024]{3,2,1,0:T(8,128)}, u32[]{:S(2)}) copy-start(f32[1,1,32,1024]{3,2,1,0:T(8,128)} %param.4) | copy-start | bytes 393220
  481.6 0.7 copy-start.2
  482.3 55.1 %reduce-scatter.2.cloned.1.call-start = ((), (), s32[]{:S(2)}) async-start(), calls=%async_computation.3 | async-start | bytes 294912 | tf_op jit(solution)/shard_map/reduce_scatter | solution.py:34
Sparse Core Ops, SparseCore 0:
  12.7 113.8 all-reduce.2
  482.4 40.5 all-gather.1
  527.6 9.7 reduce-scatter.1
where the time goes:
time: 550 us; the launch traced here: 546 us
  other arithmetic  261 us (47%)
  waiting for transfers between devices  164 us (30%)
  matrix products  57.3 us (10%)
  local copies, waits for them, and re-layouts  43.8 us (8%)
  between operations  19.7 us (4%)
    another operation x30, other arithmetic, on_device(): factor = jnp.linalg.cholesky(fisher)  168 us
    psum x1, waiting for transfers between devices, on_device(): gram_matrix = lax.psum(partial_gram, ('ex', 'pb'))  113 us
    another operation x3, other arithmetic, solve_rows(): lax.linalg.triangular_solve(factor, rows_in, left_side=False, lower=True,...  83.6 us
    all_gather x1, waiting for transfers between devices, on_device(): lax.all_gather(solved, 'ex', axis=1, tiled=True)  40.7 us
    another operation x14, matrix products, on_device(): factor = jnp.linalg.cholesky(fisher)  27.2 us
    another operation x40, local copies, waits for them, and re-layouts  23.5 us
  transfers between devices with their start and end apart: 3, of which 3 were waited for; matrix products, arithmetic and copies ran while one was open for 0% of the time, Pallas kernels for 0%

commit v1 on v0

--- a/solution.py
+++ b/solution.py
@@ -2,6 +2,28 @@
 import jax.numpy as jnp
 from jax import lax
 from jax.sharding import PartitionSpec as P
+
+
+def laid_out(blocks, dim):
+    blocks = jnp.moveaxis(blocks, 0, dim)
+    dims = blocks.shape
+    return blocks.reshape(*dims[:dim], dims[dim] * dims[dim + 1], *dims[dim + 2 :])
+
+
+def grow_blocks(array, axis):
+    size = lax.axis_size(axis)
+    blocks = array[None]
+    for level in range(size.bit_length() - 1):
+        bit = 1 << level
+        received = lax.ppermute(blocks, axis, [(i, i ^ bit) for i in range(size)])
+        both = jnp.stack([blocks, received])
+        upper = lax.axis_index(axis) >> level & 1
+        blocks = jnp.where(upper == 0, both, both[::-1]).reshape(-1, *array.shape)
+    return blocks
+
+
+def gather_by_bits(x, axis, dim):
+    return laid_out(grow_blocks(x, axis), dim)
 
 
 def solve_rows(factor, rows_in):
@@ -26,10 +48,7 @@
     queries = query_grads[:, 0]
     solved = solve_rows(factor, queries)
     score_tile = jnp.einsum(
-        "lnp,lkp->nk",
-        train_grads,
-        lax.all_gather(solved, "ex", axis=1, tiled=True),
-        precision=lax.Precision.HIGHEST,
+        "lnp,lkp->nk", train_grads, gather_by_bits(solved, "ex", 1), precision=lax.Precision.HIGHEST
     )
     shares = lax.psum_scatter(score_tile, "layer", scatter_dimension=1, tiled=True)
     return shares[:, None, :]

time: 550 us -> 578 us (1.051)
  waiting for transfers between devices: 164 us -> 189 us
    ppermute x0 -> x4, waiting for transfers between devices: none -> 65.7 us  [grow_blocks(): received = lax.ppermute(blocks, axis, [(i, i ^ bit) for i in range(size)])]
    all_gather x1 -> x0, waiting for transfers between devices: 40.7 us -> none  [on_device(): lax.all_gather(solved, 'ex', axis=1, tiled=True)]
  transfers between devices with their start and end apart: 3 -> 6, of which waited for: 3 -> 6; matrix products, arithmetic and copies ran while one was open for 0% -> 0% of each run, Pallas kernels for 0% -> 0%
where the time goes in v1:
time: 578 us; the launch traced here: 574 us
  other arithmetic  262 us (45%)
  waiting for transfers between devices  189 us (33%)
  matrix products  55.5 us (10%)
  local copies, waits for them, and re-layouts  42.9 us (7%)
  between operations  20.1 us (3%)
    another operation x30, other arithmetic, on_device(): factor = jnp.linalg.cholesky(fisher)  168 us
    psum x1, waiting for transfers between devices, on_device(): gram_matrix = lax.psum(partial_gram, ('ex', 'pb'))  113 us
    another operation x3, other arithmetic, solve_rows(): lax.linalg.triangular_solve(factor, rows_in, left_side=False, lower=True,...  83.7 us
    ppermute x4, waiting for transfers between devices, grow_blocks(): received = lax.ppermute(blocks, axis, [(i, i ^ bit) for i in range(size)])  65.7 us
    another operation x14, matrix products, on_device(): factor = jnp.linalg.cholesky(fisher)  27 us
    another operation x40, local copies, waits for them, and re-layouts  23.5 us
  transfers between devices with their start and end apart: 6, of which 6 were waited for; matrix products, arithmetic and copies ran while one was open for 0% of the time, Pallas kernels for 0%

profile of v1, /device:TPU:0, one launch (start us, length us, event | category | flops | bytes accessed | tf_op | source)
XLA Modules:
  0.0 574.2 jit_solution(7146137266213412554)
XLA Ops:
  7.5 5.0 convolution_bitcast_fusion
  13.3 113.3 %all-reduce.3.cloned.1.call-done = f32[1,1024,1024]{1,2,0:T(8,128)} async-done(((f32[1,1024,1024]{1,2,0:T(8,128)}), f32[1,1024,1024]{1,2,0:T(8,128)}) %all-reduce.3.cloned.1.call-update) | async-done | bytes 4194320 | tf_op jit(solution)/shard_map/psum | solution.py:44
  126.6 5.1 select_add_fusion
  131.7 5.8 %copy.5 = f32[1,1024,1024]{2,1,0:T(8,128)} copy(f32[1,1024,1024]{1,2,0:T(8,128)} %select_add_fusion) | data formatting | bytes 8388608 | tf_op jit(solution)/shard_map/add | solution.py:46
  137.5 4.5 fusion
  142.0 1.9 copy-done.1
  143.9 11.7 %custom-call.72 = f32[1,128,128]{2,1,0:T(8,128)S(1)} custom-call(f32[1,128,128]{2,1,0:T(8,128)S(1)} %cholesky.582), custom_call_target="Cholesky" | custom-call | tf_op jit(solution)/shard_map/jit(cholesky)/cholesky | solution.py:47
  155.8 9.8 %custom-call.73 = f32[1,1,128,128]{2,3,1,0:T(8,128)S(1)} custom-call(f32[1,1,128,128]{3,2,1,0:T(8,128)S(1)} %get-tuple-element.42), custom_call_target="InvertDiagBlocksLowerTriangular" | custom-call | tf_op jit(solution)/shard_map/jit(cholesky)/cholesky | solution.py:47
  167.3 1.5 fusion.1
  168.9 11.7 %custom-call.74 = f32[1,128,128]{2,1,0:T(8,128)S(1)} custom-call(f32[1,128,128]{2,1,0:T(8,128)S(1)} %cholesky.586), custom_call_target="Cholesky" | custom-call | tf_op jit(solution)/shard_map/jit(cholesky)/cholesky | solution.py:47
  180.9 2.5 cholesky.248
  184.2 9.8 %custom-call.75 = f32[1,1,128,128]{2,3,1,0:T(8,128)S(1)} custom-call(f32[1,1,128,128]{3,2,1,0:T(8,128)S(1)} %get-tuple-element.40), custom_call_target="InvertDiagBlocksLowerTriangular" | custom-call | tf_op jit(solution)/shard_map/jit(cholesky)/cholesky | solution.py:47
  196.0 2.7 fusion.4
  198.7 11.7 %custom-call.76 = f32[1,128,128]{2,1,0:T(8,128)S(1)} custom-call(f32[1,128,128]{2,1,0:T(8,128)S(1)} %cholesky.591), custom_call_target="Cholesky" | custom-call | tf_op jit(solution)/shard_map/jit(cholesky)/cholesky | solution.py:47
  211.2 9.8 %custom-call.77 = f32[1,1,128,128]{2,3,1,0:T(8,128)S(1)} custom-call(f32[1,1,128,128]{3,2,1,0:T(8,128)S(1)} %get-tuple-element.38), custom_call_target="InvertDiagBlocksLowerTriangular" | custom-call | tf_op jit(solution)/shard_map/jit(cholesky)/cholesky | solution.py:47
  222.2 3.3 fusion.6
  225.6 11.7 %custom-call.78 = f32[1,128,128]{2,1,0:T(8,128)S(1)} custom-call(f32[1,128,128]{2,1,0:T(8,128)S(1)} %cholesky.596), custom_call_target="Cholesky" | custom-call | tf_op jit(solution)/shard_map/jit(cholesky)/cholesky | solution.py:47
  238.1 9.8 %custom-call.79 = f32[1,1,128,128]{2,3,1,0:T(8,128)S(1)} custom-call(f32[1,1,128,128]{3,2,1,0:T(8,128)S(1)} %get-tuple-element.36), custom_call_target="InvertDiagBlocksLowerTriangular" | custom-call | tf_op jit(solution)/shard_map/jit(cholesky)/cholesky | solution.py:47
  249.0 3.1 fusion.7
  252.2 12.1 %custom-call.80 = f32[1,128,128]{2,1,0:T(8,128)S(1)} custom-call(f32[1,128,128]{2,1,0:T(8,128)S(1)} %cholesky.601), custom_call_target="Cholesky" | custom-call | tf_op jit(solution)/shard_map/jit(cholesky)/cholesky | solution.py:47
  265.0 9.8 %custom-call.81 = f32[1,1,128,128]{2,3,1,0:T(8,128)S(1)} custom-call(f32[1,1,128,128]{3,2,1,0:T(8,128)S(1)} %get-tuple-element.34), custom_call_target="InvertDiagBlocksLowerTriangular" | custom-call | tf_op jit(solution)/shard_map/jit(cholesky)/cholesky | solution.py:47
  276.0 3.1 fusion.9
  279.1 11.7 %custom-call.82 = f32[1,128,128]{2,1,0:T(8,128)S(1)} custom-call(f32[1,128,128]{2,1,0:T(8,128)S(1)} %cholesky.606), custom_call_target="Cholesky" | custom-call | tf_op jit(solution)/shard_map/jit(cholesky)/cholesky | solution.py:47
  291.6 9.8 %custom-call.83 = f32[1,1,128,128]{2,3,1,0:T(8,128)S(1)} custom-call(f32[1,1,128,128]{3,2,1,0:T(8,128)S(1)} %get-tuple-element.32), custom_call_target="InvertDiagBlocksLowerTriangular" | custom-call | tf_op jit(solution)/shard_map/jit(cholesky)/cholesky | solution.py:47
  302.4 2.8 fusion.11
  305.2 11.7 %custom-call.84 = f32[1,128,128]{2,1,0:T(8,128)S(1)} custom-call(f32[1,128,128]{2,1,0:T(8,128)S(1)} %cholesky.611), custom_call_target="Cholesky" | custom-call | tf_op jit(solution)/shard_map/jit(cholesky)/cholesky | solution.py:47
  317.7 9.8 %custom-call.85 = f32[1,1,128,128]{2,3,1,0:T(8,128)S(1)} custom-call(f32[1,1,128,128]{3,2,1,0:T(8,128)S(1)} %get-tuple-element.30), custom_call_target="InvertDiagBlocksLowerTriangular" | custom-call | tf_op jit(solution)/shard_map/jit(cholesky)/cholesky | solution.py:47
  328.4 2.1 fusion.13
  330.5 11.7 %custom-call.86 = f32[1,128,128]{2,1,0:T(8,128)S(1)} custom-call(f32[1,128,128]{2,1,0:T(8,128)S(1)} %fusion.13), custom_call_target="Cholesky" | custom-call | tf_op jit(solution)/shard_map/jit(cholesky)/cholesky | solution.py:47
  352.7 4.9 select_select_fusion
  357.6 23.7 %while.1 = (s32[]{:T(128)}, f32[1,1024,1024]{1,2,0:T(8,128)}, s32[8,2]{0,1:T(2,128)S(1)}, f32[8,1,128,128]{3,2,1,0:T(8,128)S(1)}, s32[]{:T(128)}) while((s32[]{:T(128)}, f32[1,1024,1024]{1,2,0:T(8,128)}, s32[8,2]{0,1:T(2,128)S(1)}, f32[8,1,128,128]{3,2,1,0:T(8,128)S(1)}, s32[]{:T(128)}) %tuple.50), condition=%wide.while_cond, body=%wide.while_body.sunk | while | flops 2 | bytes 393333 | solution.py:30
  358.2 2.2 constant_dynamic-slice_fusion.5
  361.2 2.2 constant_dynamic-slice_fusion.5
  364.2 2.2 constant_dynamic-slice_fusion.5
  367.2 2.2 constant_dynamic-slice_fusion.5
  370.1 2.2 constant_dynamic-slice_fusion.5
  373.1 2.2 constant_dynamic-slice_fusion.5
  376.1 2.2 constant_dynamic-slice_fusion.5
  379.1 2.2 constant_dynamic-slice_fusion.5
  381.4 78.8 %custom-call.87 = f32[1,8,128,128]{2,3,1,0:T(8,128)S(1)} custom-call(f32[1,8,128,128]{3,2,1,0:T(8,128)S(1)} %bitcast.482), custom_call_target="InvertDiagBlocksLowerTriangular" | custom-call | tf_op jit(solution)/shard_map/triangular_solve | solution.py:30
  479.6 1.6 convolution_subtract_fusion.4
  484.2 7.2 %collective-permute-done.1 = f32[2,1,32,1024]{3,2,0,1:T(8,128)S(1)} collective-permute-done((f32[2,1,32,1024]{3,2,0,1:T(8,128)S(1)}, f32[2,1,32,1024]{3,2,0,1:T(8,128)S(1)}, u32[]{:S(2)}, u32[]{:S(2)}) %collective-permute-start.1) | collective-permute-done | bytes 262176 | tf_op jit(solution)/shard_map/ppermute | solution.py:18
  492.8 11.9 %collective-permute-done.2 = f32[4,1,32,1024]{3,2,0,1:T(8,128)S(1)} collective-permute-done((f32[4,1,32,1024]{3,2,0,1:T(8,128)S(1)}, f32[4,1,32,1024]{3,2,0,1:T(8,128)S(1)}, u32[]{:S(2)}, u32[]{:S(2)}) %collective-permute-start.2) | collective-permute-done | bytes 524320 | tf_op jit(solution)/shard_map/ppermute | solution.py:18
  504.8 1.6 collective-permute-start.3
  506.5 45.3 %collective-permute-done.3 = f32[8,1,32,1024]{3,2,0,1:T(8,128)S(1)} collective-permute-done((f32[8,1,32,1024]{3,2,0,1:T(8,128)S(1)}, f32[8,1,32,1024]{3,2,0,1:T(8,128)S(1)}, u32[]{:S(2)}, u32[]{:S(2)}) %collective-permute-start.3) | collective-permute-done | bytes 1048608 | tf_op jit(solution)/shard_map/ppermute | solution.py:18
  552.3 2.8 convolution_bitcast_fusion.8
  555.2 10.3 %reduce-scatter.2.cloned.1.call-done = f32[96,256]{1,0:T(8,128)} async-done(((f32[96,512]{1,0:T(8,128)}), f32[96,256]{1,0:T(8,128)}) %reduce-scatter.2.cloned.1.call-update) | async-done | bytes 98320 | tf_op jit(solution)/shard_map/reduce_scatter | solution.py:53
  565.5 1.6 copy.22
  (153 shorter events, 50.7 us)
Async XLA Ops:
  6.5 1.0 copy-start
  6.5 120.0 %all-reduce.3.cloned.1.call-start = ((), (), s32[]{:S(2)}) async-start(), calls=%async_computation.1 | async-start | bytes 8388608 | tf_op jit(solution)/shard_map/psum | solution.py:44
  12.6 552.9 %reduce-scatter.2.cloned.1.call-start = ((), (), s32[]{:S(2)}) async-start(), calls=%async_computation.2 | async-start | bytes 294912 | tf_op jit(solution)/shard_map/reduce_scatter | solution.py:53
  142.0 1.9 copy-start.1
  352.7 107.4 %copy-start.2 = (f32[1,1,32,1024]{3,2,1,0:T(8,128)S(1)}, f32[1,1,32,1024]{3,2,1,0:T(8,128)}, u32[]{:S(2)}) copy-start(f32[1,1,32,1024]{3,2,1,0:T(8,128)} %param.4) | copy-start | bytes 393220
  481.5 1.4 collective-permute-start
  483.0 8.4 %collective-permute-start.1 = (f32[2,1,32,1024]{3,2,0,1:T(8,128)S(1)}, f32[2,1,32,1024]{3,2,0,1:T(8,128)S(1)}, u32[]{:S(2)}, u32[]{:S(2)}) collective-permute-start(f32[2,1,32,1024]{3,2,0,1:T(8,128)S(1)} %get-tuple-element.28), channel_id=1, source_target_pairs={{0,4},{2,6},{4,0},{6,2},{8,12},{10,14},{12,8},{14,10},{16,20},{18,... | collective-permute-start | bytes 786440 | tf_op jit(solution)/shard_map/ppermute | solution.py:18
  491.5 13.2 %collective-permute-start.2 = (f32[4,1,32,1024]{3,2,0,1:T(8,128)S(1)}, f32[4,1,32,1024]{3,2,0,1:T(8,128)S(1)}, u32[]{:S(2)}, u32[]{:S(2)}) collective-permute-start(f32[4,1,32,1024]{3,2,0,1:T(8,128)S(1)} %bitcast.453), channel_id=1, source_target_pairs={{0,8},{2,10},{4,12},{6,14},{8,0},{10,2},{12,4},{14,6},{16,24},{18,... | collective-permute-start | bytes 1572872 | tf_op jit(solution)/shard_map/ppermute | solution.py:18
  504.8 46.9 %collective-permute-start.3 = (f32[8,1,32,1024]{3,2,0,1:T(8,128)S(1)}, f32[8,1,32,1024]{3,2,0,1:T(8,128)S(1)}, u32[]{:S(2)}, u32[]{:S(2)}) collective-permute-start(f32[8,1,32,1024]{3,2,0,1:T(8,128)S(1)} %bitcast.450), channel_id=1, source_target_pairs={{0,16},{2,18},{4,20},{6,22},{8,24},{10,26},{12,28},{14,30},{16,0},... | collective-permute-start | bytes 3145736 | tf_op jit(solution)/shard_map/ppermute | solution.py:18
Sparse Core Ops, SparseCore 0:
  12.7 113.8 all-reduce.2
  555.3 10.1 reduce-scatter.1
